TPU v7x, 256 devices: a whole 4x4x8 slice. The times are simulated.
256 devices in a mesh: ctx: 32 (over z, x), exp: 8 (over y, core).
Axes of the slice: x: 4, y: 4, z: 8, core: 2. Of those that a mesh axis runs over, the one named last changes fastest.
Arguments:
- grad_out: bfloat16 [32768, 2880], P(('ctx', 'exp')), may hold values from -6 to 6
- top_logits: float32 [32768, 4], P(('ctx', 'exp')), may hold values from -8 to 308
- expert_ids: int32 [32768, 4], P(('ctx', 'exp')), may hold values from 0 to 7, all different within a row; in each aligned block of 128 rows (0 to 127, 128 to 255, ...) at most 96 rows name the same one
- saved_hidden: bfloat16 [32, 8, 768, 1536], P('ctx', 'exp'), may hold values from -0.29882812 to 0.29882812
- w_down: bfloat16 [8, 1536, 2880], P('exp', 'ctx'), may hold values from -0.15625 to 0.15625
Outputs:
- logit_grad: float32 [32768, 4], P(('ctx', 'exp'))
- hidden_grad: bfloat16 [32, 8, 768, 1536], P('ctx', 'exp')
- down_grad: float32 [8, 1536, 2880], P('exp', 'ctx')
Inputs may be any that keep to these rules, and one draw needn't show every extreme that they name: `expert_ids`: each row names 4 different experts; among the rows of one device no expert is named by more than 96 rows, a bound that some blocks reach.
All inputs are finite; a program needn't handle non-finite values.
Results may differ from a plain program's by a relative error of at most 0.0048.
Values may be sent and summed in bfloat16 or wider, within the bound.
A program may use at most 128 MiB of HBM per device.

v0:
```python
import jax
import jax.numpy as jnp
from jax import lax
from jax.sharding import PartitionSpec as P


def routing_tables(expert_ids, count_experts, capacity):
    columns = jnp.arange(count_experts, dtype=jnp.int32)
    matches = expert_ids[:, :, None] == columns[None, None, :]
    per_token = jnp.sum(matches.astype(jnp.int32), axis=1)
    rank_table = jnp.cumsum(per_token, axis=0) - per_token
    slot_iota = jnp.arange(capacity, dtype=jnp.int32)
    select = (per_token.T[:, None, :] == 1) & (rank_table.T[:, None, :] == slot_iota[None, :, None])
    return (matches.astype(jnp.float32), select)


def per_device(grad_out, top_logits, expert_ids, saved_hidden, w_down):
    count_experts = lax.axis_size("exp")
    slot_count = saved_hidden.shape[2]
    capacity = slot_count // count_experts
    model_width = grad_out.shape[1]
    onehot, select = routing_tables(expert_ids, count_experts, capacity)
    select_wide = select.astype(jnp.float32)
    gate_probs = jax.nn.softmax(top_logits, axis=-1)
    gate_sent = gate_probs.astype(jnp.bfloat16)
    gate_by_expert = jnp.sum(onehot * gate_sent.astype(jnp.float32)[:, :, None], axis=1)
    send_rows = jnp.einsum(
        "ect,td->ecd", select.astype(jnp.bfloat16), grad_out, preferred_element_type=jnp.float32
    ).astype(jnp.bfloat16)
    send_gate = jnp.sum(select_wide * gate_by_expert.T[:, None, :], axis=2).astype(jnp.bfloat16)
    hidden = saved_hidden[0, 0]
    rows_in, gate_in = (
        lax.all_to_all(send_rows, "exp", split_axis=0, concat_axis=0, tiled=True),
        lax.all_to_all(send_gate, "exp", split_axis=0, concat_axis=0, tiled=True),
    )
    flat_rows = rows_in.reshape(slot_count, model_width)
    backprop = lax.dot_general(
        flat_rows,
        lax.all_gather(w_down[0], "ctx", axis=0, tiled=True),
        (((1,), (1,)), ((), ())),
        preferred_element_type=jnp.float32,
    )
    flat_gate = gate_in.reshape(slot_count, 1).astype(jnp.float32)
    hidden_grad = (flat_gate * backprop).astype(jnp.bfloat16)
    slot_grad = jnp.sum(hidden.astype(jnp.float32) * backprop, axis=1)
    scaled = (flat_gate * flat_rows.astype(jnp.float32)).astype(jnp.bfloat16)
    partial_grad = lax.dot_general(
        hidden, scaled, (((0,), (0,)), ((), ())), preferred_element_type=jnp.float32
    )
    weight_grad = lax.psum_scatter(partial_grad, "ctx", scatter_dimension=0, tiled=True)
    returned = lax.all_to_all(
        slot_grad.reshape(count_experts, capacity), "exp", split_axis=0, concat_axis=0, tiled=True
    )
    grad_by_expert = jnp.sum(select_wide * returned[:, :, None], axis=1)
    gate_grad = jnp.sum(onehot * grad_by_expert.T[:, None, :], axis=2)
    logit_grad = gate_probs * (gate_grad - jnp.sum(gate_probs * gate_grad, axis=1, keepdims=True))
    return (logit_grad, hidden_grad.reshape(1, 1, slot_count, -1), weight_grad[None])


def solution(mesh):
    return jax.shard_map(
        per_device,
        mesh=mesh,
        in_specs=(
            P(("ctx", "exp"), None),
            P(("ctx", "exp"), None),
            P(("ctx", "exp"), None),
            P("ctx", "exp", None, None),
            P("exp", "ctx", None),
        ),
        out_specs=(P(("ctx", "exp"), None), P("ctx", "exp", None, None), P("exp", "ctx", None)),
        check_vma=False,
    )
```

profile of v0, /device:TPU:8, one launch (start us, length us, event | category | flops | bytes accessed | tf_op | source)
XLA Modules:
  0.0 434.2 jit_solution(5677177740942893195)
XLA Ops:
  7.2 0.0 copy-start
  7.2 0.0 all-gather.3.cloned.1.call-start
  7.2 0.7 all-gather.3.cloned.1.call-update
  7.9 0.7 convert_reduce_fusion
  8.6 0.1 copy.26
  8.7 0.2 reduce_window_sum.11
  8.9 0.0 copy-done
  9.0 3.4 convolution_convert_fusion
  12.4 6.8 %all-to-all-start = ((bf16[8,96,2880]{2,1,0:T(8,128)(2,1)}), bf16[8,96,2880]{2,1,0:T(8,128)(2,1)}, u32[]{:S(2)}, u32[]{:S(2)}) async-start(bf16[8,96,2880]{2,1,0:T(8,128)(2,1)} %convolution_convert_fusion), calls=%async_computation | async-start | bytes 9043968 | tf_op jit(solution)/shard_map/all_to_all | solution.py:33
  19.2 0.0 copy-done.2
  19.2 51.8 %all-to-all-done = bf16[8,96,2880]{2,1,0:T(8,128)(2,1)} async-done(((bf16[8,96,2880]{2,1,0:T(8,128)(2,1)}), bf16[8,96,2880]{2,1,0:T(8,128)(2,1)}, u32[]{:S(2)}, u32[]{:S(2)}) %all-to-all-start) | async-done | bytes 4423712 | tf_op jit(solution)/shard_map/all_to_all | solution.py:33
  71.0 43.6 %all-gather.3.cloned.1.call-done = bf16[1,1536,2880]{2,1,0:T(8,128)(2,1)} async-done(((bf16[1,48,2880]{2,1,0:T(8,128)(2,1)}), bf16[1,1536,2880]{2,1,0:T(8,128)(2,1)}) %all-gather.3.cloned.1.call-update) | async-done | bytes 8847376 | tf_op jit(solution)/shard_map/all_gather | solution.py:39
  114.7 0.0 copy-done.4
  114.7 13.1 %multiply_reduce_fusion = (f32[768]{0:T(1024)S(1)}, f32[768,1536]{1,0:T(8,128)}) fusion(bf16[1,1,768,1536]{3,2,1,0:T(8,128)(2,1)S(1)} %copy-done.4, bf16[768,2880]{1,0:T(8,128)(2,1)} %bitcast.4, bf16[1,1536,2880]{2,1,0:T(8,128)(2,1)} %all-gather.3.cloned.1.call-done), kind=kOutput, calls=%fused_computation.6 | convolution fusion | flops 6798310400 | bytes 20352000 | tf_op jit(solution)/shard_map/dot_general | solution.py:37
  127.8 0.7 all_to_all.14
  128.4 4.8 %all-to-all-start.1 = ((f32[8,1,96]{2,1,0:T(1,128)}), f32[8,1,96]{2,1,0:T(1,128)S(1)}, u32[]{:S(2)}, u32[]{:S(2)}) async-start(f32[8,1,96]{2,1,0:T(1,128)} %all_to_all.14), calls=%async_computation.1 | async-start | bytes 8192 | tf_op jit(solution)/shard_map/all_to_all | solution.py:51
  133.3 0.0 reduce-scatter.4.cloned.1.call-start
  133.3 0.0 copy-done.3
  133.3 3.7 all-to-all-done.1
  137.0 0.4 select_reduce_fusion
  137.4 7.7 %all_to_all.20 = bf16[8,1,96]{2,1,0:T(2,128)(2,1)S(1)} all-to-all(bf16[8,1,96]{2,1,0:T(2,128)(2,1)S(1)} %copy.29), channel_id=1, replica_groups=mesh['ctx'=32,'exp'=8] {'exp'}, dimensions={0} | all-to-all | bytes 3072 | tf_op jit(solution)/shard_map/all_to_all | solution.py:34
  145.1 3.7 multiply_convert_fusion
  148.8 10.4 %convolution_bitcast_fusion = f32[1536,2880]{0,1:T(8,128)} fusion(bf16[768,2880]{1,0:T(8,128)(2,1)S(1)} %bitcast.34, bf16[1,1,768,1536]{3,2,1,0:T(8,128)(2,1)S(1)} %copy-done.4), kind=kOutput, calls=%fused_computation | convolution fusion | flops 6794772480 | bytes 24477696 | tf_op jit(solution)/shard_map/dot_general | solution.py:47
  159.1 18.1 %copy.31 = f32[1536,2880]{1,0:T(8,128)} copy(f32[1536,2880]{0,1:T(8,128)} %convolution_bitcast_fusion) | data formatting | bytes 35389440
  177.2 0.0 reduce-scatter.4.cloned.1.call-update
  177.3 0.6 subtract_multiply_fusion
  177.9 0.1 reshape.60
  178.0 4.1 fusion.2
  182.1 242.5 %reduce-scatter.4.cloned.1.call-done = f32[48,2880]{1,0:T(8,128)} async-done(((f32[1536,2880]{1,0:T(8,128)}), f32[48,2880]{1,0:T(8,128)}) %reduce-scatter.4.cloned.1.call-update) | async-done | bytes 552976
  424.6 1.5 copy.32
  426.1 1.3 copy.30
  427.4 0.0 copy-done.1
  (16 shorter events, 0.2 us)
Async XLA Ops:
  7.2 1.8 copy-start
  7.2 107.5 %all-gather.3.cloned.1.call-start = ((), (), s32[]{:S(2)}) async-start(), calls=%async_computation.4 | async-start | bytes 9326592 | tf_op jit(solution)/shard_map/all_gather | solution.py:39
  12.4 6.8 %copy-start.2 = (f32[128,4]{0,1:T(4,128)S(1)}, f32[128,4]{0,1:T(4,128)}, u32[]{:S(2)}) copy-start(f32[128,4]{0,1:T(4,128)} %param.6) | copy-start | bytes 6148
  12.4 102.3 %copy-start.4 = (bf16[1,1,768,1536]{3,2,1,0:T(8,128)(2,1)S(1)}, bf16[1,1,768,1536]{3,2,1,0:T(8,128)(2,1)}, u32[]{:S(2)}) copy-start(bf16[1,1,768,1536]{3,2,1,0:T(8,128)(2,1)} %param.8) | copy-start | bytes 7077892
  12.4 58.6 %all-to-all-start = ((bf16[8,96,2880]{2,1,0:T(8,128)(2,1)}), bf16[8,96,2880]{2,1,0:T(8,128)(2,1)}, u32[]{:S(2)}, u32[]{:S(2)}) async-start(bf16[8,96,2880]{2,1,0:T(8,128)(2,1)} %convolution_convert_fusion), calls=%async_computation | async-start | bytes 9043968 | tf_op jit(solution)/shard_map/all_to_all | solution.py:33
  114.7 18.6 %copy-start.3 = (s32[128,4]{0,1:T(4,128)S(1)}, s32[128,4]{0,1:T(4,128)}, u32[]{:S(2)}) copy-start(s32[128,4]{0,1:T(4,128)} %param.7) | copy-start | bytes 6148
  128.4 8.6 %all-to-all-start.1 = ((f32[8,1,96]{2,1,0:T(1,128)}), f32[8,1,96]{2,1,0:T(1,128)S(1)}, u32[]{:S(2)}, u32[]{:S(2)}) async-start(f32[8,1,96]{2,1,0:T(1,128)} %all_to_all.14), calls=%async_computation.1 | async-start | bytes 8192 | tf_op jit(solution)/shard_map/all_to_all | solution.py:51
  133.3 291.3 %reduce-scatter.4.cloned.1.call-start = ((), (), s32[]{:S(2)}) async-start(), calls=%async_computation.5 | async-start | bytes 18653184
  178.0 249.4 %copy-start.1 = (bf16[128,2880]{0,1:T(8,128)(2,1)S(1)}, bf16[128,2880]{0,1:T(8,128)(2,1)}, u32[]{:S(2)}) copy-start(bf16[128,2880]{0,1:T(8,128)(2,1)} %param.5) | copy-start | bytes 2211844
Sparse Core Ops, SparseCore 0:
  10.6 104.0 all-gather.2
  177.4 247.1 reduce-scatter.3
where the time goes:
time: 435 us; the launch traced here: 434 us
  waiting for transfers between devices  342 us (79%)
  matrix products  26.9 us (6%)
  local copies, waits for them, and re-layouts  21.8 us (5%)
  between operations  14.1 us (3%)
  starting transfers between devices  11.7 us (3%)
  other arithmetic  9.78 us (2%)
  blocking collectives  7.66 us (2%)
    unnamed x3, waiting for transfers between devices  243 us
    all_to_all x1, waiting for transfers between devices, per_device(): lax.all_to_all(send_rows, 'exp', split_axis=0, concat_axis=0, tiled=True)  51.8 us
    all_gather x1, waiting for transfers between devices, per_device(): lax.all_gather(w_down[0], 'ctx', axis=0, tiled=True)  43.6 us
    unnamed x13, local copies, waits for them, and re-layouts  20.9 us
    dot_general x1, matrix products, per_device(): lax.dot_general(flat_rows, lax.all_gather(w_down[0], 'ctx', axis=0, tiled...  13.1 us
    dot_general x1, matrix products, per_device(): lax.dot_general(hidden, scaled, (((0,), (0,)), ((), ())), preferred_eleme...  10.4 us
  transfers between devices with their start and end apart: 4, of which 4 were waited for; matrix products, arithmetic and copies ran while one was open for 2% of the time, Pallas kernels for 0%

commit v1 on v0

v1 whole, which is shorter than its diff:
```python
import functools

import jax
import jax.numpy as jnp
from jax import lax
from jax.experimental import pallas as pl
from jax.experimental.pallas import tpu as pltpu
from jax.sharding import PartitionSpec as P

F32, BF16 = jnp.float32, jnp.bfloat16
LANES = 128
MESH = pl.DeviceIdType.MESH

RZ = (0, 1, -1, 2, -2, 3, -3, 4)
RX = (0, 1, -1, 2)


def out_edges(part, rz, rx):
    along_z, along_x = [], []
    if rz == 0:
        along_z = ["zF", "zR"]
    elif 0 < rz < 4:
        along_z = ["zF"]
    elif -3 < rz < 0:
        along_z = ["zR"]
    if rx == 0:
        along_x = ["xF", "xR"]
    elif rx == 1:
        along_x = ["xF"]
    if part == "A":
        return (along_x if rz == 0 else []) + along_z
    return (along_z if rx == 0 else []) + along_x


def parent_of(part, rz, rx):
    via_z = rz != 0 if part == "A" else rx == 0
    if via_z:
        return "zR" if rz > 0 else "zF"
    return "xR" if rx > 0 else "xF"


def moved(rz, rx, direction):
    step = 1 if direction[1] == "F" else -1
    return (rz + step, rx) if direction[0] == "z" else (rz, rx + step)


NODES = [(rz, rx) for rz in RZ for rx in RX]
SUM_SLOT = {}
SEND_ID = {}
for _part in "AB":
    _n = 0
    for _rz, _rx in NODES:
        for _d in out_edges(_part, _rz, _rx):
            SUM_SLOT[_part, _rz, _rx, _d] = _n
            SEND_ID[_part, _rz, _rx, _d] = _n
            _n += 1
N_EDGES = 31


def plan(bytes_a, bytes_b, bytes_half, costs, rate=85.0, hop=1.7, sibling_rate=300.0):
    size = {"A": bytes_a / 1e3, "B": bytes_b / 1e3, "y": bytes_half / 1e3}
    queues = {d: [] for d in ("zF", "zR", "xF", "xR", "yF", "yR", "ss")}
    arrivals, clock, order = [], [0.0], []
    have = set()

    def send(direction, kind, tag):
        queues[direction].append([size[kind], tag])

    def rate_of(direction):
        if direction == "ss":
            return sibling_rate
        other = direction[0] + ("R" if direction[1] == "F" else "F")
        return rate / 2 if queues[other] else rate

    def advance(until):
        while clock[0] < until - 1e-9:
            step = until - clock[0]
            for d, q in queues.items():
                if q:
                    step = min(step, q[0][0] / rate_of(d))
            rates = {d: rate_of(d) for d in queues}
            for d, q in queues.items():
                if q:
                    q[0][0] -= step * rates[d]
            clock[0] += step
            for d, q in queues.items():
                if q and q[0][0] <= 1e-6:
                    arrivals.append((clock[0] + hop, q.pop(0)[1]))

    pending = []

    def task(priority, name, needs, action=None, cost=0.1, pace=None, compute=False):
        pending.append([priority, name, frozenset(needs), action or (lambda: None), cost, pace, compute])

    def start():
        for d in ("xF", "xR"):
            send(d, "A", ("agA", *moved(0, 0, d)))
        for d in ("zF", "zR"):
            send(d, "B", ("agB", *moved(0, 0, d)))
        for d in ("xF", "xR"):
            send(d, "B", ("agB", *moved(0, 0, d)))
        for d in ("zF", "zR"):
            send(d, "A", ("agA", *moved(0, 0, d)))
        for h in (0, 1):
            send("yF", "y", ("y", 1, h))
            send("yR", "y", ("y", -1, h))
            send("ss", "y", ("s", 0, h))

    task(0, ("start",), [], start, costs["start"])

    def gather_event(part, rz, rx):
        def act():
            for d in out_edges(part, rz, rx):
                send(d, part, ("ag" + part, *moved(rz, rx, d)))
        task(1, ("ag", part, rz, rx), [("ag" + part, rz, rx)], act, 0.1)

    for part in "AB":
        for rz, rx in NODES:
            if (rz, rx) != (0, 0):
                gather_event(part, rz, rx)

    def y_event(ry, h):
        def act():
            if ry == 1:
                send("yF", "y", ("y", 2, h))
            send("ss", "y", ("s", ry, h))
        task(1, ("y", ry, h), [("y", ry, h)], act, 0.1)

    for ry in (1, -1, 2):
        for h in (0, 1):
            y_event(ry, h)
    for ry in (0, 1, -1, 2):
        for h in (0, 1):
            task(1, ("s", ry, h), [("s", ry, h)])
    task(3, ("meta",), [("done", "start")], cost=costs["meta"], compute=True)
    for i in range(costs["n_turn"]):
        task(5, ("turn", i), [("done", "meta")], cost=costs["turn"], compute=True)
    for own in (1, 0):
        for ry in (0, 1, -1, 2):
            needs = [("done", "meta")]
            if own and ry:
                needs += [("done", "y", ry, 0), ("done", "y", ry, 1)]
            if not own:
                needs += [("done", "s", ry, 0), ("done", "s", ry, 1)]
            task(4, ("sel", own, ry), needs, cost=costs["sel"], compute=True)
    sels = [("done", "sel", own, ry) for own in (1, 0) for ry in (0, 1, -1, 2)]
    turns = [("done", "turn", i) for i in range(costs["n_turn"])]
    for i, cost in enumerate(costs["pa"]):
        task(6 + 0.01 * i, ("pa", i), sels + turns, cost=cost, compute=True)
    pas = [("done", "pa", i) for i in range(len(costs["pa"]))]
    for i, cost in enumerate(costs["pb"]):
        task(7 + 0.01 * i, ("pb", i), sels + turns + pas, cost=cost, compute=True)
    pbs = [("done", "pb", i) for i in range(len(costs["pb"]))]

    def sum_event(part, rz, rx):
        kids = out_edges(part, rz, rx)
        needs = (pas if part == "A" else pbs) + [("rs" + part, rz, rx, d) for d in kids]
        towards = None if (rz, rx) == (0, 0) else parent_of(part, rz, rx)

        def act():
            if towards is not None:
                back = towards[0] + ("R" if towards[1] == "F" else "F")
                up = {"z": (rz - 1 if back[1] == "F" else rz + 1, rx), "x": (rz, rx - 1 if back[1] == "F" else rx + 1)}[back[0]]
                send(towards, part, ("rs" + part, *up, back))
        far = abs(rz) * 2 + abs(rx)
        task(1 if kids else 2 - 0.01 * far, ("rs", part, rz, rx), needs, act, 0.3 if kids else 0.05, None if kids else towards)

    for part in "AB":
        for rz, rx in NODES:
            sum_event(part, rz, rx)
    gathered = [("done", "ag", part, rz, rx) for part in "AB" for rz, rx in NODES if (rz, rx) != (0, 0)]
    for i in range(costs["n_back"]):
        task(8 + 0.01 * i, ("back", i), sels + gathered, cost=costs["back"], compute=True)
    task(2.5, ("give",), [("done", "back", i) for i in range(costs["n_back"])], cost=1.0, compute=True)
    task(9, ("logit",), [("done", "give")] + [("done", "rs", "B", rz, rx) for rz, rx in NODES[1:]], cost=1.0, compute=True)

    trace = []
    while pending:
        for a in [a for a in arrivals if a[0] <= clock[0] + 1e-9]:
            arrivals.remove(a)
            have.add(a[1])
        ready = [t for t in pending if t[2] <= have and (t[5] is None or len(queues[t[5]]) < 2)]
        if not ready:
            times = [a[0] for a in arrivals]
            nxt = min(times) if times else clock[0] + 0.5
            advance(min(nxt, clock[0] + 0.25))
            continue
        best = min(ready, key=lambda t: t[0])
        pending.remove(best)
        trace.append((round(clock[0], 2), best[1]))
        best[3]()
        advance(clock[0] + best[4])
        have.add(("done", *best[1]))
    return [name for _, name in trace], trace


def body(sizes, order, *refs):
    (n_z, n_x, n_y, tokens, width, padded, cut, shard, cap, top, experts, mm, pa_cols, pb_cols) = sizes
    (go_ref, lg_ref, ids_ref, hid_ref, w_ref, lo_ref, hg_ref, dg_ref,
     w_all, p_all, tok, rows, scl, hid_t, sum_a, sum_b, meta, ret_in, ret_out, gate, sgrad,
     ag_s, ag_r, rs_s, rs_r, y_s, y_r, sib_s, sib_r, meta_s, meta_r, ret_s, ret_r) = refs
    ctx, exp = lax.axis_index("ctx"), lax.axis_index("exp")
    z, x, y, core = ctx // n_x, ctx % n_x, exp // 2, exp % 2
    sense = 1 - 2 * core
    half = tokens // 2

    def ctx_dev(zz, xx):
        return (lax.rem(zz + 2 * n_z, n_z) * n_x + lax.rem(xx + 2 * n_x, n_x), exp)

    def exp_dev(yy, cc):
        return (ctx, lax.rem(yy + 2 * n_y, n_y) * 2 + cc)

    peer = {
        "zF": ctx_dev(z + sense, x), "zR": ctx_dev(z - sense, x),
        "xF": ctx_dev(z, x + sense), "xR": ctx_dev(z, x - sense),
        "yF": exp_dev(y + sense, core), "yR": exp_dev(y - sense, core),
        "ss": exp_dev(y, 1 - core),
    }
    others = [(ctx, lax.rem(exp + k, experts)) for k in range(1, experts)]
    barrier = pltpu.get_barrier_semaphore()
    greeted = [peer["zF"], peer["zR"], peer["xF"], peer["xR"]] + others
    for dev in greeted:
        pl.semaphore_signal(barrier, inc=1, device_id=dev, device_id_type=MESH)

    def shard_rows(rz, rx):
        zz = lax.rem(z - sense * rz + 2 * n_z, n_z)
        xx = lax.rem(x - sense * rx + 2 * n_x, n_x)
        return pl.ds(pl.multiple_of((zz * n_x + xx) * shard, shard), shard)

    cols = {"A": pl.ds(0, cut), "B": pl.ds(cut, padded - cut)}
    sums = {"A": sum_a, "B": sum_b}
    which = {"A": 0, "B": 1}
    sends = []

    def remote(src, dst, s_sem, r_sem, dev):
        return pltpu.make_async_remote_copy(
            src_ref=src, dst_ref=dst, send_sem=s_sem, recv_sem=r_sem, device_id=dev, device_id_type=MESH
        )

    def push(*args):
        copy = remote(*args)
        copy.start()
        sends.append(copy)

    def gather_recv_sem(part, rz, rx):
        return ag_r.at[which[part], NODES.index((rz, rx))]

    def gather_pass(part, rz, rx, directions):
        ref = w_all.at[shard_rows(rz, rx), cols[part]]
        for d in directions:
            push(ref, ref, ag_s.at[which[part], SEND_ID[part, rz, rx, d]], gather_recv_sem(part, *moved(rz, rx, d)), peer[d])

    def gather_event(part, rz, rx):
        ref = w_all.at[shard_rows(rz, rx), cols[part]]
        remote(ref, ref, ag_s.at[0, 0], gather_recv_sem(part, rz, rx), peer["zF"]).wait_recv()
        gather_pass(part, rz, rx, out_edges(part, rz, rx))

    Y_INDEX = {0: 0, 1: 1, -1: 2, 2: 3}

    def block_of(own, ry):
        yy = lax.rem(y - sense * ry + 2 * n_y, n_y) if own else lax.rem(y + sense * ry + 2 * n_y, n_y)
        return yy * 2 + (core if own else 1 - core)

    def half_ref(own, ry, h):
        return tok.at[block_of(own, ry), pl.ds(h * half, half)]

    def y_push(ry, h, d):
        ref = half_ref(True, ry, h)
        to = ry + (1 if d == "yF" else -1)
        push(ref, ref, y_s.at[{"yF": ry, "yR": 2}[d], h], y_r.at[Y_INDEX[to], h], peer[d])

    def sib_push(ry, h):
        ref = half_ref(True, ry, h)
        push(ref, ref, sib_s.at[Y_INDEX[ry], h], sib_r.at[Y_INDEX[ry], h], peer["ss"])

    def y_event(ry, h):
        ref = half_ref(True, ry, h)
        remote(ref, ref, y_s.at[0, 0], y_r.at[Y_INDEX[ry], h], peer["yF"]).wait_recv()
        if ry == 1:
            y_push(1, h, "yF")
        sib_push(ry, h)

    def s_event(ry, h):
        ref = half_ref(False, ry, h)
        remote(ref, ref, y_s.at[0, 0], sib_r.at[Y_INDEX[ry], h], peer["ss"]).wait_recv()

    def start():
        tail = width // LANES * LANES
        me = block_of(True, 0)
        tok[me, :, pl.ds(tail, padded - tail)] = jnp.zeros((tokens, padded - tail), BF16)
        tok[me, :, pl.ds(0, width)] = go_ref[...]
        mine = shard_rows(0, 0)
        w_all[mine, pl.ds(tail, padded - tail)] = jnp.zeros((shard, padded - tail), BF16)
        w_all[mine, pl.ds(0, width)] = w_ref[...]
        pl.semaphore_wait(barrier, len(greeted))
        gather_pass("A", 0, 0, ["xF", "xR"])
        gather_pass("B", 0, 0, ["zF", "zR"])
        gather_pass("B", 0, 0, ["xF", "xR"])
        gather_pass("A", 0, 0, ["zF", "zR"])
        for h in (0, 1):
            y_push(0, h, "yF")
            y_push(0, h, "yR")
            sib_push(0, h)

    def gate_probs():
        logits = lg_ref[...]
        weights = jnp.exp(logits - jnp.max(logits, axis=1, keepdims=True))
        return weights / jnp.sum(weights, axis=1, keepdims=True)

    def matches():
        lane = lax.broadcasted_iota(jnp.int32, (tokens, LANES), 1)
        ids = ids_ref[...]
        return [ids[:, k:k + 1] == lane for k in range(top)]

    def meta_task():
        sent = gate_probs().astype(BF16).astype(F32)
        chosen = jnp.zeros((tokens, LANES), F32)
        by_expert = jnp.zeros((tokens, LANES), F32)
        for k, match in enumerate(matches()):
            chosen = chosen + jnp.where(match, 1.0, 0.0)
            by_expert = by_expert + jnp.where(match, sent[:, k:k + 1], 0.0)
        earlier = lax.broadcasted_iota(jnp.int32, (tokens, tokens), 0) > lax.broadcasted_iota(jnp.int32, (tokens, tokens), 1)
        rank = jnp.dot(jnp.where(earlier, 1.0, 0.0).astype(BF16), chosen.astype(BF16), preferred_element_type=F32)
        rank = jnp.where(chosen > 0.5, rank, -1.0)
        meta[exp, pl.ds(0, experts), :] = rank.T[0:experts, :]
        meta[exp, pl.ds(experts, experts), :] = by_expert.T[0:experts, :]

    def meta_send():
        for k in range(1, experts):
            push(meta.at[exp], meta.at[exp], meta_s.at[k - 1], meta_r.at[k - 1], others[k - 1])

    def meta_wait():
        for k in range(1, experts):
            src = lax.rem(exp - k + experts, experts)
            remote(meta.at[src], meta.at[src], meta_s.at[0], meta_r.at[k - 1], others[0]).wait_recv()

    def select_of(s):
        rank = meta[s, pl.ds(exp, 1), :]
        slot = lax.broadcasted_iota(jnp.int32, (cap, tokens), 0).astype(F32)
        return rank == slot

    def sel_task(own, ry):
        s = block_of(own, ry)
        select = select_of(s)
        gates = jnp.sum(jnp.where(select, meta[s, pl.ds(experts + exp, 1), :], 0.0), axis=1, keepdims=True)
        at = pl.ds(pl.multiple_of(s * cap, cap), cap)
        gate[at, :] = jnp.broadcast_to(gates, (cap, LANES))
        picked = jnp.dot(jnp.where(select, 1.0, 0.0).astype(BF16), tok[s], preferred_element_type=F32)
        rows[at, :] = picked.astype(BF16)
        scl[at, :] = (gates * picked).astype(BF16)

    slots = experts * cap
    n_f = hid_ref.shape[1]

    def turn_task(i):
        span = n_f // mm["n_turn"]
        hid_t[pl.ds(i * span, span), :] = hid_ref[:, pl.ds(i * span, span)].T

    def grad_cols(at, span):
        p_all[:, pl.ds(at, span)] = jnp.dot(hid_t[...], scl[:, pl.ds(at, span)], preferred_element_type=F32).astype(BF16)

    def grad_task(base, count, span):
        if count == 1:
            grad_cols(base, span)
            return

        def step(i, _):
            grad_cols(pl.multiple_of(base + i * span, LANES), span)
            return 0
        lax.fori_loop(0, count, step, 0)

    def sum_event(part, rz, rx):
        kids = out_edges(part, rz, rx)
        mine = p_all.at[shard_rows(rz, rx), cols[part]]
        src = mine
        if kids:
            total = mine[...].astype(F32)
            for d in kids:
                slot = SUM_SLOT[part, rz, rx, d]
                ref = sums[part].at[slot]
                remote(ref, ref, rs_s.at[0, 0], rs_r.at[which[part], slot], peer["zF"]).wait_recv()
                total = total + ref[...].astype(F32)
            if (rz, rx) == (0, 0):
                if part == "A":
                    dg_ref[:, pl.ds(0, cut)] = total
                else:
                    dg_ref[:, pl.ds(cut, width - cut)] = total[:, 0:width - cut]
                return
            src = sums[part].at[SUM_SLOT[part, rz, rx, kids[0]]]
            src[...] = total.astype(BF16)
        towards = parent_of(part, rz, rx)
        back = towards[0] + ("R" if towards[1] == "F" else "F")
        step = -1 if back[1] == "F" else 1
        up = (rz + step, rx) if back[0] == "z" else (rz, rx + step)
        slot = SUM_SLOT[part, *up, back]
        push(src, sums[part].at[slot], rs_s.at[which[part], slot], rs_r.at[which[part], slot], peer[towards])

    def back_cols(at, span, first):
        prod = lax.dot_general(rows[...], w_all[pl.ds(at, span), :], (((1,), (1,)), ((), ())), preferred_element_type=F32)
        hg_ref[:, pl.ds(at, span)] = (gate[:, 0:1] * prod).astype(BF16)
        weighted = hid_ref[:, pl.ds(at, span)].astype(F32) * prod
        part = weighted[:, 0:LANES]
        for j in range(1, span // LANES):
            part = part + weighted[:, j * LANES:(j + 1) * LANES]
        sgrad[...] = part if first else sgrad[...] + part

    def back_task(i):
        span = n_f // mm["n_back"]
        back_cols(i * span, span, i == 0)

    def give_task():
        for k in range(experts):
            s = lax.rem(exp + k, experts)
            total = jnp.sum(sgrad[pl.ds(pl.multiple_of(s * cap, cap), cap), :], axis=1, keepdims=True)
            row = jnp.sum(jnp.where(select_of(s), total, 0.0), axis=0, keepdims=True)
            if k == 0:
                ret_in[exp] = jnp.broadcast_to(row, (8, tokens))
            else:
                ret_out[k - 1] = jnp.broadcast_to(row, (8, tokens))
        for k in range(1, experts):
            push(ret_out.at[k - 1], ret_in.at[exp], ret_s.at[k - 1], ret_r.at[k - 1], others[k - 1])

    def logit_task():
        for k in range(1, experts):
            src = lax.rem(exp - k + experts, experts)
            remote(ret_in.at[src], ret_in.at[src], ret_s.at[0], ret_r.at[k - 1], others[0]).wait_recv()
        by_expert = jnp.concatenate(
            [ret_in[e, 0:1, :] for e in range(experts)] + [jnp.zeros((tokens - experts, tokens), F32)], axis=0
        ).T
        probs = gate_probs()
        grads = [jnp.sum(jnp.where(m, by_expert, 0.0), axis=1, keepdims=True) for m in matches()]
        mean = sum(probs[:, k:k + 1] * g for k, g in enumerate(grads))
        for k, g in enumerate(grads):
            lo_ref[:, k:k + 1] = probs[:, k:k + 1] * (g - mean)

    sent_meta = [False, False]
    for name in order:
        kind = name[0]
        if kind == "start":
            start()
        elif kind == "meta":
            meta_task()
        elif kind == "ag":
            gather_event(*name[1:])
        elif kind == "y":
            y_event(*name[1:])
        elif kind == "s":
            s_event(*name[1:])
        elif kind == "turn":
            turn_task(name[1])
            if not sent_meta[0]:
                meta_send()
                sent_meta[0] = True
        elif kind == "sel":
            if not sent_meta[0]:
                meta_send()
                sent_meta[0] = True
            if not sent_meta[1] and name[1:] != (1, 0):
                meta_wait()
                sent_meta[1] = True
            sel_task(*name[1:])
        elif kind == "pa":
            grad_task(*pa_cols[name[1]])
        elif kind == "pb":
            grad_task(*pb_cols[name[1]])
        elif kind == "rs":
            sum_event(*name[1:])
        elif kind == "back":
            back_task(name[1])
        elif kind == "give":
            give_task()
        elif kind == "logit":
            logit_task()
    for copy in sends:
        copy.wait_send()


def per_device(grad_out, top_logits, expert_ids, saved_hidden, w_down):
    n_z, n_x, n_y = 8, 4, 4
    tokens, width = grad_out.shape
    slots, n_f = saved_hidden.shape[2:]
    shard = w_down.shape[1]
    top = top_logits.shape[1]
    experts = n_y * 2
    cap = slots // experts
    padded = -(-width // LANES) * LANES
    cut = padded * 9 // 23 // LANES * LANES
    span = 256

    def pieces(base, end, groups):
        whole = (end - base) // span
        out = []
        at = base
        for g in range(groups):
            count = whole * (g + 1) // groups - whole * g // groups
            if count:
                out.append((at, count, span))
                at += count * span
        if at < end:
            out.append((at, 1, end - at))
        return out

    pa_cols, pb_cols = pieces(0, cut, 2), pieces(cut, padded, 3)
    mm = {"n_turn": 6, "n_back": 6}
    chunk = 1.0
    costs = {
        "start": 0.5, "meta": 1.5, "turn": 0.6, "n_turn": mm["n_turn"], "sel": 0.9,
        "pa": [chunk * c for _, c, _ in pa_cols], "pb": [chunk * c for _, c, _ in pb_cols],
        "back": 2.0, "n_back": mm["n_back"],
    }
    order, _ = plan(shard * cut * 2, shard * (padded - cut) * 2, tokens // 2 * padded * 2, costs)
    sizes = (n_z, n_x, n_y, tokens, width, padded, cut, shard, cap, top, experts, mm, pa_cols, pb_cols)
    vmem = pl.BlockSpec(memory_space=pltpu.VMEM)
    dma = pltpu.SemaphoreType.DMA
    logit, hidden_grad, down_grad = pl.pallas_call(
        functools.partial(body, sizes, order),
        out_shape=(
            jax.ShapeDtypeStruct((tokens, top), F32),
            jax.ShapeDtypeStruct((slots, n_f), BF16),
            jax.ShapeDtypeStruct((shard, width), F32),
        ),
        in_specs=[vmem] * 5,
        out_specs=(vmem, vmem, vmem),
        scratch_shapes=[
            pltpu.VMEM((n_f, padded), BF16),
            pltpu.VMEM((n_f, padded), BF16),
            pltpu.VMEM((experts, tokens, padded), BF16),
            pltpu.VMEM((slots, padded), BF16),
            pltpu.VMEM((slots, padded), BF16),
            pltpu.VMEM((n_f, slots), BF16),
            pltpu.VMEM((N_EDGES, shard, cut), BF16),
            pltpu.VMEM((N_EDGES, shard, padded - cut), BF16),
            pltpu.VMEM((experts, 2 * experts, tokens), F32),
            pltpu.VMEM((experts, 8, tokens), F32),
            pltpu.VMEM((experts, 8, tokens), F32),
            pltpu.VMEM((slots, LANES), F32),
            pltpu.VMEM((slots, LANES), F32),
            dma((2, N_EDGES)), dma((2, len(NODES))),
            dma((2, N_EDGES)), dma((2, N_EDGES)),
            dma((3, 2)), dma((4, 2)), dma((4, 2)), dma((4, 2)),
            dma((experts - 1,)), dma((experts - 1,)), dma((experts - 1,)), dma((experts - 1,)),
        ],
        compiler_params=pltpu.CompilerParams(collective_id=0, has_side_effects=True, vmem_limit_bytes=63000 * 1024),
    )(grad_out, top_logits, expert_ids, saved_hidden[0, 0], w_down[0])
    return (logit, hidden_grad[None, None], down_grad[None])


def solution(mesh):
    return jax.shard_map(
        per_device,
        mesh=mesh,
        in_specs=(
            P(("ctx", "exp"), None),
            P(("ctx", "exp"), None),
            P(("ctx", "exp"), None),
            P("ctx", "exp", None, None),
            P("exp", "ctx", None),
        ),
        out_specs=(P(("ctx", "exp"), None), P("ctx", "exp", None, None), P("exp", "ctx", None)),
        check_vma=False,
    )
```

time: 435 us -> 146 us (0.34)
  waiting for transfers between devices: 342 us -> 0 us
  Pallas kernels: 0 us -> 134 us
  matrix products: 26.9 us -> 0 us
  between operations: 14.1 us -> 0.64 us
  starting transfers between devices: 11.7 us -> 0 us
  local copies, waits for them, and re-layouts: 21.8 us -> 10.7 us
  other arithmetic: 9.78 us -> 0 us
  blocking collectives: 7.66 us -> 0 us
    unnamed x3 -> x0, waiting for transfers between devices: 243 us -> none
    pallas_call x0 -> x1, Pallas kernels: none -> 134 us  [per_device(): pl.pallas_call(functools.partial(body, sizes, order), out_shape=(jax.Shap...]
    all_to_all x2 -> x0, waiting for transfers between devices: 55.5 us -> none  [the longest x1 51.8 us: per_device(): lax.all_to_all(send_rows, 'exp', split_axis=0, concat_axis=0, tiled=True)]
    all_gather x1 -> x0, waiting for transfers between devices: 43.6 us -> none  [per_device(): lax.all_gather(w_down[0], 'ctx', axis=0, tiled=True)]
    dot_general x3 -> x0, matrix products: 26.9 us -> none  [the longest x1 13.1 us: per_device(): lax.dot_general(flat_rows, lax.all_gather(w_down[0], 'ctx', axis=0, tiled...]
    all_to_all x2 -> x0, starting transfers between devices: 11.6 us -> none  [the longest x1 6.81 us: per_device(): lax.all_to_all(send_rows, 'exp', split_axis=0, concat_axis=0, tiled=True)]
    unnamed x13 -> x8, local copies, waits for them, and re-layouts: 20.9 us -> 10.7 us
    all_to_all x1 -> x0, blocking collectives: 7.66 us -> none  [per_device(): lax.all_to_all(send_gate, 'exp', split_axis=0, concat_axis=0, tiled=True)]
  transfers between devices with their start and end apart: 4 -> 0, of which waited for: 4 -> 0; matrix products, arithmetic and copies ran while one was open for 2% -> 0% of each run, Pallas kernels for 0% -> 0%
where the time goes in v1:
time: 146 us; the launch traced here: 145 us
  Pallas kernels  134 us (92%)
  local copies, waits for them, and re-layouts  10.7 us (7%)
    pallas_call x1, Pallas kernels, per_device(): pl.pallas_call(functools.partial(body, sizes, order), out_shape=(jax.Shap...  134 us
    unnamed x8, local copies, waits for them, and re-layouts  10.7 us

profile of v1, /device:TPU:8, one launch (start us, length us, event | category | flops | bytes accessed | tf_op | source)
XLA Modules:
  0.0 145.3 jit_solution(8120858676611395518)
XLA Ops:
  0.6 1.4 copy.9.refs_1_
  2.0 1.4 copy.10.refs_2_
  3.4 2.3 %copy.8.refs_0_ = bf16[128,2880]{1,0:T(8,128)(2,1)} copy(bf16[128,2880]{0,1:T(8,128)(2,1)} %param.5) | data formatting | bytes 1474560 | tf_op args[0]
  5.7 134.0 %shard_map.76 = (f32[128,4]{1,0:T(8,128)}, bf16[768,1536]{1,0:T(8,128)(2,1)}, f32[48,2880]{1,0:T(8,128)}) custom-call(bf16[128,2880]{1,0:T(8,128)(2,1)} %copy.8.refs_0_, f32[128,4]{1,0:T(8,128)} %copy.9.refs_1_, s32[128,4]{1,0:T(8,128)} %copy.10.refs_2_, bf16[768,1536]{1,0:T(8,128)(2,1)} %bitcast.4, bf16[48,2880]{1,0:T(8,128)(2,1)} %bitcast.7), custom_call_target="tpu_custom_call" | custom-call | tf_op jit(solution)/shard_map/pallas_call | solution.py:515
  139.7 1.5 %copy.11 = f32[128,4]{0,1:T(4,128)} copy(f32[128,4]{1,0:T(8,128)} %get-tuple-element.9) | data formatting | bytes 4096
  141.2 0.0 copy-start
  141.2 3.3 %copy.14 = bf16[1,1,768,1536]{3,2,1,0:T(8,128)(2,1)} copy(bf16[1,1,768,1536]{3,2,1,0:T(8,128)(2,1)} %bitcast.5) | data formatting | bytes 4718592
  144.5 0.0 copy-done
  144.5 0.8 copy.15
Async XLA Ops:
  141.2 3.3 %copy-start = (f32[48,2880]{1,0:T(8,128)S(1)}, f32[48,2880]{1,0:T(8,128)}, u32[]{:S(2)}) copy-start(f32[48,2880]{1,0:T(8,128)} %get-tuple-element.8) | copy-start | bytes 1658884

commit v2 on v0

v2 whole, which is shorter than its diff:
```python
import functools

import jax
import jax.numpy as jnp
from jax import lax
from jax.experimental import pallas as pl
from jax.experimental.pallas import tpu as pltpu
from jax.sharding import PartitionSpec as P

F32, BF16 = jnp.float32, jnp.bfloat16
LANES = 128
MESH = pl.DeviceIdType.MESH

RZ = (0, 1, -1, 2, -2, 3, -3, 4)
RX = (0, 1, -1, 2)


def out_edges(part, rz, rx):
    along_z, along_x = [], []
    if rz == 0:
        along_z = ["zF", "zR"]
    elif 0 < rz < 4:
        along_z = ["zF"]
    elif -3 < rz < 0:
        along_z = ["zR"]
    if rx == 0:
        along_x = ["xF", "xR"]
    elif rx == 1:
        along_x = ["xF"]
    if part == "A":
        return (along_x if rz == 0 else []) + along_z
    return (along_z if rx == 0 else []) + along_x


def parent_of(part, rz, rx):
    via_z = rz != 0 if part == "A" else rx == 0
    if via_z:
        return "zR" if rz > 0 else "zF"
    return "xR" if rx > 0 else "xF"


def moved(rz, rx, direction):
    step = 1 if direction[1] == "F" else -1
    return (rz + step, rx) if direction[0] == "z" else (rz, rx + step)


NODES = [(rz, rx) for rz in RZ for rx in RX]
SUM_SLOT = {}
SEND_ID = {}
for _part in "AB":
    _n = 0
    for _rz, _rx in NODES:
        for _d in out_edges(_part, _rz, _rx):
            SUM_SLOT[_part, _rz, _rx, _d] = _n
            SEND_ID[_part, _rz, _rx, _d] = _n
            _n += 1
N_EDGES = 31


def sum_target(part, rz, rx):
    towards = parent_of(part, rz, rx)
    back = towards[0] + ("R" if towards[1] == "F" else "F")
    step = -1 if back[1] == "F" else 1
    up = (rz + step, rx) if back[0] == "z" else (rz, rx + step)
    return towards, SUM_SLOT[part, *up, back]


def task_list(n_turn, n_pa, n_pb, n_back):
    out = [("start",), ("meta",), ("msend",), ("mwait",), ("give",), ("logit",)]
    for part in "AB":
        for rz, rx in NODES:
            if (rz, rx) != (0, 0):
                out.append(("aw", part, rz, rx))
            out += [("ap", part, rz, rx, d) for d in out_edges(part, rz, rx)]
    for part in "AB":
        for rz, rx in NODES:
            if out_edges(part, rz, rx):
                out.append(("rs", part, rz, rx))
            if (rz, rx) != (0, 0):
                out.append(("rp", part, rz, rx))
    for h in (0, 1):
        out += [("yp", 0, h, "yF"), ("yp", 0, h, "yR"), ("yp", 0, h, "ss")]
        for ry in (1, -1, 2):
            out.append(("yw", ry, h))
            out.append(("yp", ry, h, "ss"))
        out.append(("yp", 1, h, "yF"))
        out += [("sw", ry, h) for ry in (0, 1, -1, 2)]
    for own in (1, 0):
        out += [("sel", own, ry) for ry in (0, 1, -1, 2)]
    out += [("turn", i) for i in range(n_turn)]
    out += [("pa", i) for i in range(n_pa)]
    out += [("pb", i) for i in range(n_pb)]
    out += [("back", i) for i in range(n_back)]
    return out


ORDER = [
    0, 70, 69, 233, 71, 232, 234, 7, 1, 2, 248, 6, 68, 9, 247, 8, 260, 242, 268, 269, 270, 271, 256, 272,
    84, 87, 85, 86, 273, 246, 72, 73, 74, 3, 264, 28, 29, 76, 78, 77, 79, 10, 12, 13, 14, 16, 15, 11,
    20, 237, 238, 100, 103, 235, 236, 241, 101, 21, 88, 90, 244, 44, 45, 89, 243, 92, 93, 95, 30, 31, 75, 82,
    22, 23, 94, 32, 251, 252, 249, 255, 262, 33, 24, 25, 80, 81, 261, 106, 250, 258, 266, 36, 116, 118, 17, 19,
    239, 18, 240, 117, 257, 265, 98, 60, 245, 37, 108, 111, 91, 46, 47, 110, 253, 254, 263, 109, 38, 121, 48, 49,
    259, 267, 96, 97, 274, 39, 40, 275, 34, 35, 114, 102, 276, 83, 26, 27, 277, 61, 278, 119, 120, 182, 184, 279,
    52, 280, 53, 62, 112, 113, 183, 281, 282, 99, 50, 123, 125, 124, 181, 177, 283, 104, 105, 284, 171, 54, 55, 51,
    285, 207, 225, 122, 219, 172, 212, 175, 42, 43, 128, 176, 173, 115, 64, 178, 231, 230, 174, 169, 161, 162, 204, 126,
    213, 170, 63, 41, 127, 65, 222, 155, 58, 59, 107, 156, 223, 218, 159, 163, 164, 160, 216, 217, 157, 145, 158, 206,
    146, 228, 56, 57, 153, 154, 229, 188, 139, 67, 140, 179, 210, 129, 143, 147, 211, 144, 148, 224, 141, 142, 180, 201,
    194, 137, 66, 138, 286, 287, 165, 200, 195, 288, 289, 226, 205, 227, 290, 167, 168, 291, 220, 221, 189, 4, 214, 215,
    166, 151, 152, 198, 199, 208, 209, 192, 193, 5, 149, 150, 202, 135, 203, 136, 186, 187, 133, 196, 197, 134, 190, 191,
    131, 132, 185, 130,
]


def body(sizes, order, *refs):
    (n_z, n_x, n_y, tokens, width, padded, cut, shard, cap, top, experts, spans) = sizes
    turns, pa_cols, pb_cols, backs = spans
    (go_hbm, lg_ref, ids_ref, hid_hbm, w_hbm, lo_ref, hg_hbm, dg_hbm,
     w_all, p_all, tok, rows, scl, hid, hid_t, hg, sum_a, sum_b, meta, ret_in, ret_out, gate, sgrad, go_ref, dg_ref,
     ag_s, ag_r, rs_s, rs_r, y_s, y_r, sib_s, sib_r, meta_s, meta_r, ret_s, ret_r, in_sem, hg_sem, dg_sem) = refs
    ctx, exp = lax.axis_index("ctx"), lax.axis_index("exp")
    z, x, y, core = ctx // n_x, ctx % n_x, exp // 2, exp % 2
    sense = 1 - 2 * core
    half = width // 2

    def ctx_dev(zz, xx):
        return (lax.rem(zz + 2 * n_z, n_z) * n_x + lax.rem(xx + 2 * n_x, n_x), exp)

    def exp_dev(yy, cc):
        return (ctx, lax.rem(yy + 2 * n_y, n_y) * 2 + cc)

    peer = {
        "zF": ctx_dev(z + sense, x), "zR": ctx_dev(z - sense, x),
        "xF": ctx_dev(z, x + sense), "xR": ctx_dev(z, x - sense),
        "yF": exp_dev(y + sense, core), "yR": exp_dev(y - sense, core),
        "ss": exp_dev(y, 1 - core),
    }
    others = [(ctx, lax.rem(exp + k, experts)) for k in range(1, experts)]
    slots = experts * cap
    barrier = pltpu.get_barrier_semaphore()
    greeted = [peer["zF"], peer["zR"], peer["xF"], peer["xR"]] + others
    for dev in greeted:
        pl.semaphore_signal(barrier, inc=1, device_id=dev, device_id_type=MESH)

    def shard_rows(rz, rx):
        zz = lax.rem(z - sense * rz + 2 * n_z, n_z)
        xx = lax.rem(x - sense * rx + 2 * n_x, n_x)
        return pl.ds(pl.multiple_of((zz * n_x + xx) * shard, shard), shard)

    cols = {"A": pl.ds(0, cut), "B": pl.ds(cut, padded - cut)}
    sums = {"A": sum_a, "B": sum_b}
    which = {"A": 0, "B": 1}
    sends = []

    def remote(src, dst, s_sem, r_sem, dev):
        return pltpu.make_async_remote_copy(
            src_ref=src, dst_ref=dst, send_sem=s_sem, recv_sem=r_sem, device_id=dev, device_id_type=MESH
        )

    def push(*args):
        copy = remote(*args)
        copy.start()
        sends.append(copy)

    def gather_recv_sem(part, rz, rx):
        return ag_r.at[which[part], NODES.index((rz, rx))]

    def gather_pass(part, rz, rx, d):
        ref = w_all.at[shard_rows(rz, rx), cols[part]]
        push(ref, ref, ag_s.at[which[part], SEND_ID[part, rz, rx, d]], gather_recv_sem(part, *moved(rz, rx, d)), peer[d])

    def gather_wait(part, rz, rx):
        ref = w_all.at[shard_rows(rz, rx), cols[part]]
        remote(ref, ref, ag_s.at[0, 0], gather_recv_sem(part, rz, rx), peer["zF"]).wait_recv()

    Y_INDEX = {0: 0, 1: 1, -1: 2, 2: 3}

    def block_of(own, ry):
        yy = lax.rem(y - sense * ry + 2 * n_y, n_y) if own else lax.rem(y + sense * ry + 2 * n_y, n_y)
        return yy * 2 + (core if own else 1 - core)

    def half_ref(own, ry, h):
        return tok.at[block_of(own, ry), pl.ds(h * half, half)]

    def y_push(ry, h, d):
        ref = half_ref(True, ry, h)
        src = go_ref.at[pl.ds(h * half, half)] if ry == 0 else ref
        if d == "ss":
            push(src, ref, sib_s.at[Y_INDEX[ry], h], sib_r.at[Y_INDEX[ry], h], peer["ss"])
            return
        to = ry + (1 if d == "yF" else -1)
        push(src, ref, y_s.at[{"yF": ry, "yR": 2}[d], h], y_r.at[Y_INDEX[to], h], peer[d])

    def y_wait(ry, h):
        ref = half_ref(True, ry, h)
        remote(ref, ref, y_s.at[0, 0], y_r.at[Y_INDEX[ry], h], peer["yF"]).wait_recv()

    def s_wait(ry, h):
        ref = half_ref(False, ry, h)
        remote(ref, ref, y_s.at[0, 0], sib_r.at[Y_INDEX[ry], h], peer["ss"]).wait_recv()

    loads = {
        "w": pltpu.make_async_copy(w_hbm, w_all.at[shard_rows(0, 0)], in_sem.at[0]),
        "go": pltpu.make_async_copy(go_hbm, go_ref, in_sem.at[1]),
        "hid": pltpu.make_async_copy(hid_hbm, hid, in_sem.at[2]),
    }

    def start():
        for name in ("w", "go", "hid"):
            loads[name].start()
        loads["w"].wait()
        loads["go"].wait()
        pl.semaphore_wait(barrier, len(greeted))

    def store_down_grad(i):
        at = (pl.ds(0, cut), pl.ds(cut, width - cut))[i]
        return pltpu.make_async_copy(dg_ref.at[:, at], dg_hbm.at[:, at], dg_sem.at[i])

    def gate_probs():
        logits = lg_ref[...]
        weights = jnp.exp(logits - jnp.max(logits, axis=0, keepdims=True))
        return weights / jnp.sum(weights, axis=0, keepdims=True)

    def matches():
        row = lax.broadcasted_iota(jnp.int32, (experts, tokens), 0)
        ids = ids_ref[...]
        return [ids[k:k + 1, :] == row for k in range(top)]

    def meta_task():
        sent = gate_probs().astype(BF16).astype(F32)
        chosen = jnp.zeros((experts, tokens), F32)
        by_expert = jnp.zeros((experts, tokens), F32)
        for k, match in enumerate(matches()):
            chosen = chosen + jnp.where(match, 1.0, 0.0)
            by_expert = by_expert + jnp.where(match, sent[k:k + 1, :], 0.0)
        earlier = lax.broadcasted_iota(jnp.int32, (tokens, tokens), 0) < lax.broadcasted_iota(jnp.int32, (tokens, tokens), 1)
        rank = jnp.dot(chosen.astype(BF16), jnp.where(earlier, 1.0, 0.0).astype(BF16), preferred_element_type=F32)
        meta[exp, pl.ds(0, experts), :] = jnp.where(chosen > 0.5, rank, -1.0)
        meta[exp, pl.ds(experts, experts), :] = by_expert

    def meta_send():
        for k in range(1, experts):
            push(meta.at[exp], meta.at[exp], meta_s.at[k - 1], meta_r.at[k - 1], others[k - 1])

    def meta_wait():
        for k in range(1, experts):
            src = lax.rem(exp - k + experts, experts)
            remote(meta.at[src], meta.at[src], meta_s.at[0], meta_r.at[k - 1], others[0]).wait_recv()

    def select_of(s):
        rank = meta[s, pl.ds(exp, 1), :]
        slot = lax.broadcasted_iota(jnp.int32, (cap, tokens), 0).astype(F32)
        return rank == slot

    def sel_task(own, ry):
        s = block_of(own, ry)
        select = select_of(s)
        gates = jnp.sum(jnp.where(select, meta[s, pl.ds(experts + exp, 1), :], 0.0), axis=1, keepdims=True)
        at = pl.ds(pl.multiple_of(s * cap, cap), cap)
        gate[at, :] = jnp.broadcast_to(gates, (cap, LANES))
        block = go_ref[...] if own and ry == 0 else tok[s]
        picked = lax.dot_general(
            jnp.where(select, 1.0, 0.0).astype(BF16), block, (((1,), (1,)), ((), ())), preferred_element_type=F32
        )
        rows[at, pl.ds(0, width)] = picked.astype(BF16)
        scl[at, pl.ds(0, width)] = (gates * picked).astype(BF16)

    def turn_task(at, span):
        hid_t[pl.ds(at, span), :] = hid[:, pl.ds(at, span)].T

    def grad_cols(at, span):
        p_all[:, pl.ds(at, span)] = jnp.dot(hid_t[...], scl[:, pl.ds(at, span)], preferred_element_type=F32).astype(BF16)

    def partial_ref(part, rz, rx):
        return p_all.at[shard_rows(rz, rx), cols[part]]

    def sum_task(part, rz, rx):
        kids = out_edges(part, rz, rx)
        total = partial_ref(part, rz, rx)[...].astype(F32)
        for d in kids:
            slot = SUM_SLOT[part, rz, rx, d]
            ref = sums[part].at[slot]
            remote(ref, ref, rs_s.at[0, 0], rs_r.at[which[part], slot], peer["zF"]).wait_recv()
            total = total + ref[...].astype(F32)
        if (rz, rx) != (0, 0):
            sums[part][SUM_SLOT[part, rz, rx, kids[0]]] = total.astype(BF16)
        elif part == "A":
            dg_ref[:, pl.ds(0, cut)] = total
            store_down_grad(0).start()
        else:
            dg_ref[:, pl.ds(cut, width - cut)] = total
            store_down_grad(1).start()

    def sum_push(part, rz, rx):
        kids = out_edges(part, rz, rx)
        src = sums[part].at[SUM_SLOT[part, rz, rx, kids[0]]] if kids else partial_ref(part, rz, rx)
        towards, slot = sum_target(part, rz, rx)
        push(src, sums[part].at[slot], rs_s.at[which[part], slot], rs_r.at[which[part], slot], peer[towards])

    def store_hidden_grad(i):
        at, span = backs[i]
        return pltpu.make_async_copy(hg.at[:, pl.ds(at, span)], hg_hbm.at[:, pl.ds(at, span)], hg_sem.at[i])

    def back_task(i):
        at, span = backs[i]
        prod = lax.dot_general(rows[...], w_all[pl.ds(at, span), :], (((1,), (1,)), ((), ())), preferred_element_type=F32)
        hg[:, pl.ds(at, span)] = (gate[:, 0:1] * prod).astype(BF16)
        weighted = hid[:, pl.ds(at, span)].astype(F32) * prod
        part = weighted[:, 0:LANES]
        for j in range(1, span // LANES):
            part = part + weighted[:, j * LANES:(j + 1) * LANES]
        sgrad[...] = part if i == 0 else sgrad[...] + part
        if i:
            store_hidden_grad(i - 1).start()
        if i == len(backs) - 1:
            store_hidden_grad(i).start()

    def give_task():
        for k in range(experts):
            s = lax.rem(exp + k, experts)
            total = jnp.sum(sgrad[pl.ds(pl.multiple_of(s * cap, cap), cap), :], axis=1, keepdims=True)
            row = jnp.sum(jnp.where(select_of(s), total, 0.0), axis=0, keepdims=True)
            if k == 0:
                ret_in[exp] = jnp.broadcast_to(row, (8, tokens))
            else:
                ret_out[k - 1] = jnp.broadcast_to(row, (8, tokens))
        for k in range(1, experts):
            push(ret_out.at[k - 1], ret_in.at[exp], ret_s.at[k - 1], ret_r.at[k - 1], others[k - 1])

    def logit_task():
        for k in range(1, experts):
            src = lax.rem(exp - k + experts, experts)
            remote(ret_in.at[src], ret_in.at[src], ret_s.at[0], ret_r.at[k - 1], others[0]).wait_recv()
        by_expert = jnp.concatenate([ret_in[e, 0:1, :] for e in range(experts)], axis=0)
        probs = gate_probs()
        grads = jnp.concatenate([jnp.sum(jnp.where(m, by_expert, 0.0), axis=0, keepdims=True) for m in matches()], axis=0)
        lo_ref[...] = probs * (grads - jnp.sum(probs * grads, axis=0, keepdims=True))

    emit = {
        "start": start, "meta": meta_task, "msend": meta_send, "mwait": meta_wait, "give": give_task, "logit": logit_task,
        "aw": gather_wait, "ap": gather_pass, "rs": sum_task, "rp": sum_push, "yp": y_push, "yw": y_wait, "sw": s_wait,
        "sel": sel_task, "pa": lambda i: grad_cols(*pa_cols[i]), "pb": lambda i: grad_cols(*pb_cols[i]),
        "turn": lambda i: turn_task(*turns[i]), "back": back_task,
    }
    for name in order:
        if name == ("turn", 0):
            loads["hid"].wait()
        emit[name[0]](*name[1:])
    for i in range(len(backs)):
        store_hidden_grad(i).wait()
    for i in (0, 1):
        store_down_grad(i).wait()
    for copy in sends:
        copy.wait_send()


def hand_on(parts, *refs):
    n = len(parts)
    srcs, dsts, bufs, (in_sem, out_sem) = refs[:n], refs[n:2 * n], refs[2 * n:3 * n], refs[3 * n:]
    pieces = [(a, pl.ds(i * size, size)) for a, (count, size) in enumerate(parts) for i in range(count)]
    loads = [pltpu.make_async_copy(srcs[a].at[at], bufs[a].at[at], in_sem.at[k]) for k, (a, at) in enumerate(pieces)]
    stores = [pltpu.make_async_copy(bufs[a].at[at], dsts[a].at[at], out_sem.at[k]) for k, (a, at) in enumerate(pieces)]
    for load in loads:
        load.start()
    for load, store in zip(loads, stores):
        load.wait()
        store.start()
    for store in stores:
        store.wait()


def handed_on(*arrays):
    parts = [(8, a.shape[0] // 8) if a.shape[0] >= 512 else (1, a.shape[0]) for a in arrays]
    total = sum(count for count, _ in parts)
    hbm = pl.BlockSpec(memory_space=pl.ANY)
    return pl.pallas_call(
        functools.partial(hand_on, parts),
        out_shape=tuple(jax.ShapeDtypeStruct(a.shape, a.dtype) for a in arrays),
        in_specs=[hbm] * len(arrays),
        out_specs=(hbm,) * len(arrays),
        scratch_shapes=[pltpu.VMEM(a.shape, a.dtype) for a in arrays]
        + [pltpu.SemaphoreType.DMA((total,)), pltpu.SemaphoreType.DMA((total,))],
    )(*arrays)


def per_device(grad_out, top_logits, expert_ids, saved_hidden, w_down):
    n_z, n_x, n_y = 8, 4, 4
    tokens, width = grad_out.shape
    hbm = pl.BlockSpec(memory_space=pl.ANY)
    slots, n_f = saved_hidden.shape[2:]
    shard = w_down.shape[1]
    top = top_logits.shape[1]
    experts = n_y * 2
    cap = slots // experts
    padded = width
    cut = padded * 2 // 5 // LANES * LANES

    def pieces(base, end, span=256):
        return [(at, min(span, end - at)) for at in range(base, end, span)]

    spans = (pieces(0, n_f), pieces(0, cut), pieces(cut, padded), pieces(0, n_f))
    tasks = task_list(*(len(p) for p in spans))
    order = [tasks[i] for i in ORDER]
    sizes = (n_z, n_x, n_y, tokens, width, padded, cut, shard, cap, top, experts, spans)
    vmem = pl.BlockSpec(memory_space=pltpu.VMEM)
    dma = pltpu.SemaphoreType.DMA
    logit, hidden_grad, down_grad = pl.pallas_call(
        functools.partial(body, sizes, order),
        out_shape=(
            jax.ShapeDtypeStruct((top, tokens), F32),
            jax.ShapeDtypeStruct((slots, n_f), BF16),
            jax.ShapeDtypeStruct((shard, width), F32),
        ),
        in_specs=[hbm, vmem, vmem, hbm, hbm],
        out_specs=(vmem, hbm, hbm),
        scratch_shapes=[
            pltpu.VMEM((n_f, padded), BF16),
            pltpu.VMEM((n_f, padded), BF16),
            pltpu.VMEM((experts, width, tokens), BF16),
            pltpu.VMEM((slots, padded), BF16),
            pltpu.VMEM((slots, padded), BF16),
            pltpu.VMEM((slots, n_f), BF16),
            pltpu.VMEM((n_f, slots), BF16),
            pltpu.VMEM((slots, n_f), BF16),
            pltpu.VMEM((N_EDGES, shard, cut), BF16),
            pltpu.VMEM((N_EDGES, shard, padded - cut), BF16),
            pltpu.VMEM((experts, 2 * experts, tokens), F32),
            pltpu.VMEM((experts, 8, tokens), F32),
            pltpu.VMEM((experts, 8, tokens), F32),
            pltpu.VMEM((slots, LANES), F32),
            pltpu.VMEM((slots, LANES), F32),
            pltpu.VMEM((width, tokens), BF16),
            pltpu.VMEM((shard, width), F32),
            dma((2, N_EDGES)), dma((2, len(NODES))),
            dma((2, N_EDGES)), dma((2, N_EDGES)),
            dma((3, 2)), dma((4, 2)), dma((4, 2)), dma((4, 2)),
            dma((experts - 1,)), dma((experts - 1,)), dma((experts - 1,)), dma((experts - 1,)), dma((3,)), dma((len(spans[3]),)), dma((2,)),
        ],
        compiler_params=pltpu.CompilerParams(collective_id=0, has_side_effects=True, vmem_limit_bytes=63000 * 1024),
    )(grad_out.T, top_logits.T, expert_ids.T, saved_hidden[0, 0], w_down[0])
    logit, hidden_grad, down_grad = handed_on(logit, hidden_grad, down_grad)
    return (logit.T, hidden_grad[None, None], down_grad[None])


def solution(mesh):
    return jax.shard_map(
        per_device,
        mesh=mesh,
        in_specs=(
            P(("ctx", "exp"), None),
            P(("ctx", "exp"), None),
            P(("ctx", "exp"), None),
            P("ctx", "exp", None, None),
            P("exp", "ctx", None),
        ),
        out_specs=(P(("ctx", "exp"), None), P("ctx", "exp", None, None), P("exp", "ctx", None)),
        check_vma=False,
    )
```

time: 435 us -> 123 us (0.28)
  waiting for transfers between devices: 342 us -> 0 us
  Pallas kernels: 0 us -> 120 us
  matrix products: 26.9 us -> 0 us
  local copies, waits for them, and re-layouts: 21.8 us -> 0 us
  between operations: 14.1 us -> 0.8 us
  starting transfers between devices: 11.7 us -> 0 us
  other arithmetic: 9.78 us -> 0 us
  blocking collectives: 7.66 us -> 0 us
    unnamed x3 -> x0, waiting for transfers between devices: 243 us -> none
    pallas_call x0 -> x2, Pallas kernels: none -> 120 us  [the longest x1 117 us: per_device(): pl.pallas_call(functools.partial(body, sizes, order), out_shape=(jax.Shap...]
    all_to_all x2 -> x0, waiting for transfers between devices: 55.5 us -> none  [the longest x1 51.8 us: per_device(): lax.all_to_all(send_rows, 'exp', split_axis=0, concat_axis=0, tiled=True)]
    all_gather x1 -> x0, waiting for transfers between devices: 43.6 us -> none  [per_device(): lax.all_gather(w_down[0], 'ctx', axis=0, tiled=True)]
    dot_general x3 -> x0, matrix products: 26.9 us -> none  [the longest x1 13.1 us: per_device(): lax.dot_general(flat_rows, lax.all_gather(w_down[0], 'ctx', axis=0, tiled...]
    unnamed x13 -> x0, local copies, waits for them, and re-layouts: 20.9 us -> none
    all_to_all x2 -> x0, starting transfers between devices: 11.6 us -> none  [the longest x1 6.81 us: per_device(): lax.all_to_all(send_rows, 'exp', split_axis=0, concat_axis=0, tiled=True)]
    all_to_all x1 -> x0, blocking collectives: 7.66 us -> none  [per_device(): lax.all_to_all(send_gate, 'exp', split_axis=0, concat_axis=0, tiled=True)]
  transfers between devices with their start and end apart: 4 -> 0, of which waited for: 4 -> 0; matrix products, arithmetic and copies ran while one was open for 2% -> 0% of each run, Pallas kernels for 0% -> 0%
where the time goes in v2:
time: 123 us; the launch traced here: 121 us
  Pallas kernels  120 us (98%)
    pallas_call x1, Pallas kernels, per_device(): pl.pallas_call(functools.partial(body, sizes, order), out_shape=(jax.Shap...  117 us
    pallas_call x1, Pallas kernels, handed_on(): pl.pallas_call(functools.partial(hand_on, parts), out_shape=tuple((jax.Sh...  2.76 us

profile of v2, /device:TPU:8, one launch (start us, length us, event | category | flops | bytes accessed | tf_op | source)
XLA Modules:
  0.0 120.6 jit_solution(15491226431907200954)
XLA Ops:
  0.6 117.0 %shard_map.76 = (f32[4,128]{1,0:T(4,128)}, bf16[768,1536]{1,0:T(8,128)(2,1)}, f32[48,2880]{1,0:T(8,128)}) custom-call(bf16[2880,128]{1,0:T(8,128)(2,1)} %bitcast.9, f32[4,128]{1,0:T(4,128)} %bitcast.11, s32[4,128]{1,0:T(4,128)} %bitcast.12, bf16[768,1536]{1,0:T(8,128)(2,1)} %bitcast.8, bf16[48,2880]{1,0:T(8,128)(2,1)} %bitcast.10), custom_call_target="tpu_custom_call" | custom-call | tf_op jit(solution)/shard_map/pallas_call | solution.py:406
  117.7 2.8 %shard_map.77 = (f32[4,128]{1,0:T(4,128)}, bf16[768,1536]{1,0:T(8,128)(2,1)}, f32[48,2880]{1,0:T(8,128)}) custom-call(f32[4,128]{1,0:T(4,128)} %get-tuple-element.9.refs_0_, bf16[768,1536]{1,0:T(8,128)(2,1)} %get-tuple-element.10.refs_1_, f32[48,2880]{1,0:T(8,128)} %get-tuple-element.11.refs_2_), custom_call_target="tpu_custom_call" | custom-call | tf_op jit(solution)/shard_map/pallas_call | solution.py:375

commit v3 on v2

--- a/solution.py
+++ b/solution.py
@@ -66,7 +66,7 @@
 
 
 def task_list(n_turn, n_pa, n_pb, n_back):
-    out = [("start",), ("meta",), ("msend",), ("mwait",), ("give",), ("logit",)]
+    out = [("start",), ("msend",), ("mwait",), ("give",), ("logit",)]
     for part in "AB":
         for rz, rx in NODES:
             if (rz, rx) != (0, 0):
@@ -95,19 +95,19 @@
 
 
 ORDER = [
-    0, 70, 69, 233, 71, 232, 234, 7, 1, 2, 248, 6, 68, 9, 247, 8, 260, 242, 268, 269, 270, 271, 256, 272,
-    84, 87, 85, 86, 273, 246, 72, 73, 74, 3, 264, 28, 29, 76, 78, 77, 79, 10, 12, 13, 14, 16, 15, 11,
-    20, 237, 238, 100, 103, 235, 236, 241, 101, 21, 88, 90, 244, 44, 45, 89, 243, 92, 93, 95, 30, 31, 75, 82,
-    22, 23, 94, 32, 251, 252, 249, 255, 262, 33, 24, 25, 80, 81, 261, 106, 250, 258, 266, 36, 116, 118, 17, 19,
-    239, 18, 240, 117, 257, 265, 98, 60, 245, 37, 108, 111, 91, 46, 47, 110, 253, 254, 263, 109, 38, 121, 48, 49,
-    259, 267, 96, 97, 274, 39, 40, 275, 34, 35, 114, 102, 276, 83, 26, 27, 277, 61, 278, 119, 120, 182, 184, 279,
-    52, 280, 53, 62, 112, 113, 183, 281, 282, 99, 50, 123, 125, 124, 181, 177, 283, 104, 105, 284, 171, 54, 55, 51,
-    285, 207, 225, 122, 219, 172, 212, 175, 42, 43, 128, 176, 173, 115, 64, 178, 231, 230, 174, 169, 161, 162, 204, 126,
-    213, 170, 63, 41, 127, 65, 222, 155, 58, 59, 107, 156, 223, 218, 159, 163, 164, 160, 216, 217, 157, 145, 158, 206,
-    146, 228, 56, 57, 153, 154, 229, 188, 139, 67, 140, 179, 210, 129, 143, 147, 211, 144, 148, 224, 141, 142, 180, 201,
-    194, 137, 66, 138, 286, 287, 165, 200, 195, 288, 289, 226, 205, 227, 290, 167, 168, 291, 220, 221, 189, 4, 214, 215,
-    166, 151, 152, 198, 199, 208, 209, 192, 193, 5, 149, 150, 202, 135, 203, 136, 186, 187, 133, 196, 197, 134, 190, 191,
-    131, 132, 185, 130,
+    0, 5, 68, 6, 67, 1, 233, 231, 70, 69, 232, 7, 246, 245, 259, 247, 241, 8, 9, 10, 11, 13, 14, 255,
+    15, 83, 85, 86, 75, 76, 77, 78, 84, 71, 72, 27, 73, 19, 20, 16, 17, 31, 21, 22, 234, 240, 235, 236,
+    237, 32, 89, 23, 242, 87, 88, 24, 99, 101, 100, 102, 243, 81, 47, 91, 92, 79, 94, 93, 48, 35, 36, 248,
+    254, 249, 267, 268, 269, 270, 271, 272, 2, 263, 260, 250, 251, 261, 74, 18, 115, 105, 117, 25, 256, 26, 264, 80,
+    257, 265, 12, 61, 238, 239, 37, 38, 90, 97, 116, 28, 33, 244, 39, 252, 253, 40, 262, 34, 103, 104, 29, 120,
+    258, 266, 273, 107, 95, 96, 43, 108, 110, 30, 274, 109, 275, 82, 51, 52, 276, 49, 277, 183, 176, 278, 118, 41,
+    279, 119, 280, 45, 281, 53, 181, 42, 282, 113, 106, 283, 284, 55, 174, 224, 223, 229, 175, 56, 230, 218, 98, 111,
+    180, 54, 170, 122, 123, 124, 46, 178, 158, 63, 121, 221, 112, 159, 179, 222, 168, 160, 169, 161, 60, 57, 227, 211,
+    228, 171, 58, 142, 65, 215, 193, 143, 177, 152, 64, 212, 125, 153, 154, 164, 127, 165, 126, 194, 155, 166, 167, 114,
+    219, 220, 44, 205, 144, 136, 216, 145, 50, 66, 138, 225, 217, 206, 226, 162, 59, 163, 209, 148, 62, 149, 187, 200,
+    139, 150, 128, 285, 191, 151, 182, 210, 286, 287, 137, 288, 289, 172, 146, 213, 203, 173, 147, 204, 290, 134, 197, 135,
+    198, 214, 3, 188, 199, 207, 208, 192, 156, 157, 201, 202, 130, 131, 140, 141, 195, 196, 185, 186, 189, 190, 132, 133,
+    4, 129, 184,
 ]
 
 
@@ -166,7 +166,8 @@
 
     def gather_pass(part, rz, rx, d):
         ref = w_all.at[shard_rows(rz, rx), cols[part]]
-        push(ref, ref, ag_s.at[which[part], SEND_ID[part, rz, rx, d]], gather_recv_sem(part, *moved(rz, rx, d)), peer[d])
+        src = w_hbm.at[:, cols[part]] if (rz, rx) == (0, 0) else ref
+        push(src, ref, ag_s.at[which[part], SEND_ID[part, rz, rx, d]], gather_recv_sem(part, *moved(rz, rx, d)), peer[d])
 
     def gather_wait(part, rz, rx):
         ref = w_all.at[shard_rows(rz, rx), cols[part]]
@@ -183,7 +184,7 @@
 
     def y_push(ry, h, d):
         ref = half_ref(True, ry, h)
-        src = go_ref.at[pl.ds(h * half, half)] if ry == 0 else ref
+        src = go_hbm.at[pl.ds(h * half, half)] if ry == 0 else ref
         if d == "ss":
             push(src, ref, sib_s.at[Y_INDEX[ry], h], sib_r.at[Y_INDEX[ry], h], peer["ss"])
             return
@@ -207,8 +208,7 @@
     def start():
         for name in ("w", "go", "hid"):
             loads[name].start()
-        loads["w"].wait()
-        loads["go"].wait()
+        meta_task()
         pl.semaphore_wait(barrier, len(greeted))
 
     def store_down_grad(i):
@@ -336,7 +336,7 @@
         lo_ref[...] = probs * (grads - jnp.sum(probs * grads, axis=0, keepdims=True))
 
     emit = {
-        "start": start, "meta": meta_task, "msend": meta_send, "mwait": meta_wait, "give": give_task, "logit": logit_task,
+        "start": start, "msend": meta_send, "mwait": meta_wait, "give": give_task, "logit": logit_task,
         "aw": gather_wait, "ap": gather_pass, "rs": sum_task, "rp": sum_push, "yp": y_push, "yw": y_wait, "sw": s_wait,
         "sel": sel_task, "pa": lambda i: grad_cols(*pa_cols[i]), "pb": lambda i: grad_cols(*pb_cols[i]),
         "turn": lambda i: turn_task(*turns[i]), "back": back_task,
@@ -344,6 +344,10 @@
     for name in order:
         if name == ("turn", 0):
             loads["hid"].wait()
+        if name == ("sel", 1, 0):
+            loads["go"].wait()
+        if name == ("back", 0):
+            loads["w"].wait()
         emit[name[0]](*name[1:])
     for i in range(len(backs)):
         store_hidden_grad(i).wait()

time: 123 us -> 121 us (0.984); the launches traced: 121 us -> 121 us
  no operation moved by 1% of the time
where the time goes in v3:
time: 121 us
  Pallas kernels  120 us (99%)
    pallas_call x1, Pallas kernels, per_device(): pl.pallas_call(functools.partial(body, sizes, order), out_shape=(jax.Shap...  117 us
    pallas_call x1, Pallas kernels, handed_on(): pl.pallas_call(functools.partial(hand_on, parts), out_shape=tuple((jax.Sh...  2.76 us

profile of v3, /device:TPU:8, one launch (start us, length us, event | category | flops | bytes accessed | tf_op | source)
XLA Modules:
  0.0 120.8 jit_solution(847056553986090713)
XLA Ops:
  0.6 117.3 %shard_map.76 = (f32[4,128]{1,0:T(4,128)}, bf16[768,1536]{1,0:T(8,128)(2,1)}, f32[48,2880]{1,0:T(8,128)}) custom-call(bf16[2880,128]{1,0:T(8,128)(2,1)} %bitcast.9, f32[4,128]{1,0:T(4,128)} %bitcast.11, s32[4,128]{1,0:T(4,128)} %bitcast.12, bf16[768,1536]{1,0:T(8,128)(2,1)} %bitcast.8, bf16[48,2880]{1,0:T(8,128)(2,1)} %bitcast.10), custom_call_target="tpu_custom_call" | custom-call | tf_op jit(solution)/shard_map/pallas_call | solution.py:410
  117.9 2.8 %shard_map.77 = (f32[4,128]{1,0:T(4,128)}, bf16[768,1536]{1,0:T(8,128)(2,1)}, f32[48,2880]{1,0:T(8,128)}) custom-call(f32[4,128]{1,0:T(4,128)} %get-tuple-element.9.refs_0_, bf16[768,1536]{1,0:T(8,128)(2,1)} %get-tuple-element.10.refs_1_, f32[48,2880]{1,0:T(8,128)} %get-tuple-element.11.refs_2_), custom_call_target="tpu_custom_call" | custom-call | tf_op jit(solution)/shard_map/pallas_call | solution.py:379
